TPU v7x, 256 devices: a whole 4x4x8 slice. The times are simulated.
256 devices in a mesh: ctx: 8 (over x, y_hi), chan: 32 (over z, y_lo, core).
Axes of the slice: x: 4, y: 4 (y_hi: 2, y_lo: 2; y = y_hi * 2 + y_lo), z: 8, core: 2. Of those that a mesh axis runs over, the one named last changes fastest.
Arguments:
- inputs: bfloat16 [4096, 4096], P('ctx', 'chan'), may hold values from -6 to 6
- w_in: bfloat16 [4096, 3, 4096], P(None, None, 'chan'), may hold values from -0.09375 to 0.09375
- conv_taps: bfloat16 [3, 3, 4096], P(None, None, 'chan'), may hold values from -3.59375 to 3.59375
- skip_gain: float32 [4096], P('chan'), may hold values from 0.5 to 1.5
- filter_taps: bfloat16 [4096, 4096], P('ctx', 'chan'), may hold values from -0.09375 to 0.09375
- w_out: bfloat16 [4096, 4096], P('chan'), may hold values from -0.1875 to 0.1875
Outputs:
- result: bfloat16 [4096, 4096], P('ctx', 'chan')
All inputs are finite; a program needn't handle non-finite values.
Results may differ from a plain program's by a relative error of at most 0.024.
Values may be sent and summed in bfloat16 or wider, within the bound.
A program may use at most 64 MiB of HBM per device.

v0:
```python
import math
import jax
import jax.numpy as jnp
from jax import lax
from jax.sharding import PartitionSpec as P

KERNEL = 3


def dft_table(double_len):
    step = 32
    hi_ids = jnp.arange(double_len // step, dtype=jnp.int32)[:, None]
    lo_ids = jnp.arange(step, dtype=jnp.int32)[:, None]
    cols = jnp.arange(double_len, dtype=jnp.int32)[None, :]
    scale = 2.0 * math.pi / double_len
    hi_angle = scale * (hi_ids * step * cols % double_len).astype(jnp.float32)
    lo_angle = scale * (lo_ids * cols % double_len).astype(jnp.float32)
    hc, hs = (jnp.cos(hi_angle)[:, None], jnp.sin(hi_angle)[:, None])
    lc, ls = (jnp.cos(lo_angle)[None], jnp.sin(lo_angle)[None])
    cos = (hc * lc - hs * ls).reshape(double_len, double_len)
    sin = (hs * lc + hc * ls).reshape(double_len, double_len)
    return jnp.concatenate([cos, -sin], 0).astype(jnp.bfloat16)


def body(inputs, w_in, conv_taps, skip_gain, filter_taps, w_out):
    span_len, width_dev = inputs.shape
    double_len = 2 * span_len
    groups = lax.axis_size("ctx")
    position = lax.axis_index("ctx")
    own = width_dev // groups
    with jax.named_scope("out_weight_columns"):
        w_cols = lax.all_to_all(w_out, "chan", 1, 0, tiled=True)
    with jax.named_scope("filter_to_owner"):
        taps_t = filter_taps.T.reshape(groups, own, span_len)
        taps_t = lax.all_to_all(taps_t, "ctx", 0, 0, tiled=True)
    with jax.named_scope("input_projection"):
        inputs_t = lax.all_gather(inputs.T, "chan", axis=0, tiled=True)
        w_flat = w_in.reshape(w_in.shape[0], 3 * width_dev)
        proj_t = lax.dot_general(
            w_flat, inputs_t, (((0,), (0,)), ((), ())), preferred_element_type=jnp.float32
        ).astype(jnp.bfloat16)
    with jax.named_scope("projection_to_owner"):
        proj_t = proj_t.reshape(3, groups, own, span_len)
        proj_t = lax.all_to_all(proj_t, "ctx", 1, 1, tiled=True)
    with jax.named_scope("short_conv"):
        start = position * own
        taps = lax.dynamic_slice_in_dim(conv_taps, start, own, axis=2)
        rim = jnp.pad(
            proj_t[:, :-1, :, span_len - (KERNEL - 1) :], ((0, 0), (1, 0), (0, 0), (0, 0))
        )
        padded = jnp.concatenate([rim, proj_t], 3)
        filtered = jnp.zeros(proj_t.shape, jnp.float32)
        for lag in range(KERNEL):
            start_row = KERNEL - 1 - lag
            filtered = filtered + taps[lag].astype(jnp.float32)[:, None, :, None] * padded[
                ..., start_row : start_row + span_len
            ].astype(jnp.float32)
        streams = filtered.astype(jnp.bfloat16)
        gate_out = streams[0]
        gated_in = (streams[1].astype(jnp.float32) * streams[2].astype(jnp.float32)).astype(
            jnp.bfloat16
        )
    with jax.named_scope("spectra"):
        table = dft_table(double_len)
        forward_in = table[:, :span_len]
        spectra_in = jnp.einsum(
            "jdb,fb->jdf", gated_in, forward_in, preferred_element_type=jnp.float32
        ).astype(jnp.bfloat16)
        previous = jnp.pad(taps_t[:-1, :, 1:], ((1, 0), (0, 0), (0, 0)))
        padded_taps = jnp.concatenate(
            [taps_t, jnp.zeros((groups, own, 1), jnp.bfloat16), previous], 2
        )
        spectra_taps = jnp.einsum(
            "kdm,fm->kdf", padded_taps, table, preferred_element_type=jnp.float32
        ).astype(jnp.bfloat16)
    with jax.named_scope("mixture"):
        real_g = spectra_taps[:, :, :double_len].astype(jnp.float32)
        imag_g = spectra_taps[:, :, double_len:].astype(jnp.float32)
        real_u = spectra_in[:, :, :double_len].astype(jnp.float32)
        imag_u = spectra_in[:, :, double_len:].astype(jnp.float32)
        mixed = []
        for target in range(groups):
            acc_r = jnp.zeros((own, double_len), jnp.float32)
            acc_i = jnp.zeros((own, double_len), jnp.float32)
            for source in range(target + 1):
                lag = target - source
                acc_r = acc_r + (real_g[lag] * real_u[source] - imag_g[lag] * imag_u[source])
                acc_i = acc_i + (real_g[lag] * imag_u[source] + imag_g[lag] * real_u[source])
            mixed.append(jnp.concatenate([acc_r, acc_i], 1))
        mixture = jnp.stack(mixed, 0).astype(jnp.bfloat16)
    with jax.named_scope("inverse_and_gate"):
        long_out = jnp.einsum(
            "idf,fa->ida", mixture, forward_in, preferred_element_type=jnp.float32
        ) * (1.0 / double_len)
        gain = lax.dynamic_slice_in_dim(skip_gain, start, own)
        long_out = long_out + gain[None, :, None] * gated_in.astype(jnp.float32)
        gated_out = (gate_out.astype(jnp.float32) * long_out).astype(jnp.bfloat16)
    with jax.named_scope("gated_back_to_rows"):
        gated_out = lax.all_to_all(gated_out, "ctx", 0, 0, tiled=True)
        gated_out = gated_out.reshape(width_dev, span_len)
    with jax.named_scope("output_projection"):
        gathered = lax.all_gather(gated_out, "chan", axis=0, tiled=True)
        result = lax.dot_general(
            gathered, w_cols, (((0,), (0,)), ((), ())), preferred_element_type=jnp.float32
        ).astype(jnp.bfloat16)
    return result


def solution(mesh):
    return jax.shard_map(
        body,
        mesh=mesh,
        in_specs=(
            P("ctx", "chan"),
            P(None, None, "chan"),
            P(None, None, "chan"),
            P("chan"),
            P("ctx", "chan"),
            P("chan", None),
        ),
        out_specs=P("ctx", "chan"),
        check_vma=False,
    )
```

profile of v0, /device:TPU:1, one launch (start us, length us, event | category | flops | bytes accessed | tf_op | source)
XLA Modules:
  0.0 208.1 jit_solution(4928286048202900547)
XLA Ops:
  6.5 0.0 copy-start
  6.5 0.0 all-gather.3.cloned.1.call-start
  6.5 0.7 all-gather.3.cloned.1.call-update
  7.3 1.9 copy.19
  9.1 7.5 %all-to-all-start.1 = ((bf16[8,16,512]{2,1,0:T(8,128)(2,1)}), bf16[8,16,512]{2,1,0:T(8,128)(2,1)S(1)}, u32[]{:S(2)}, u32[]{:S(2)}) async-start(bf16[8,16,512]{2,1,0:T(8,128)(2,1)} %bitcast.8), calls=%async_computation.1 | async-start | bytes 262144 | tf_op jit(solution)/shard_map/filter_to_owner/all_to_all | solution.py:35
  16.6 0.5 fusion.45
  17.2 0.6 fusion.48
  17.8 3.5 %negate_convert_fusion = (bf16[32,32,1024]{2,1,0:T(8,128)(2,1)}, bf16[32,32,1024]{2,1,0:T(8,128)(2,1)}) fusion(f32[32,1024]{1,0:T(8,128)S(1)} %get-tuple-element.22, f32[32,1024]{1,0:T(8,128)S(1)} %get-tuple-element.21, f32[32,1024]{1,0:T(8,128)S(1)} %get-tuple-element.23, f32[32,1024]{1,0:T(8,128)S(1)} %get-tuple-element.20), kind=kLoop, calls=%fused_computation.5 | loop fusion | flops 9437184 | bytes 4718592 | tf_op jit(solution)/shard_map/convert.44
  21.3 0.0 copy-start.6
  21.3 0.0 copy-start.5
  21.3 0.0 copy-done
  21.3 2.9 %copy.14 = bf16[4096,3,128]{0,2,1:T(8,128)(2,1)} copy(bf16[4096,3,128]{2,0,1:T(8,128)(2,1)S(1)} %copy-done) | data formatting | bytes 6291456 | tf_op args[1]
  24.2 0.0 copy-done.6
  24.2 0.1 dynamic_slice.7
  24.3 0.0 copy-done.5
  24.3 0.1 fusion.68
  24.3 0.0 all-to-all-done.1
  24.4 0.0 copy-start.4
  24.4 0.1 slice.145
  24.5 61.2 %all-gather.3.cloned.1.call-done = bf16[4096,512]{0,1:T(8,128)(2,1)} async-done(((bf16[128,512]{0,1:T(8,128)(2,1)}), bf16[4096,512]{0,1:T(8,128)(2,1)}) %all-gather.3.cloned.1.call-update) | async-done | bytes 4194320 | tf_op jit(solution)/shard_map/input_projection/all_gather | solution.py:37
  85.6 0.0 copy-start.1
  85.6 5.1 %convolution_convert_fusion.1 = bf16[384,512]{1,0:T(8,128)(2,1)S(1)} fusion(bf16[4096,384]{0,1:T(8,128)(2,1)} %bitcast.117, bf16[4096,512]{0,1:T(8,128)(2,1)} %all-gather.3.cloned.1.call-done), kind=kOutput, calls=%fused_computation.11 | convolution fusion | flops 1610809344 | bytes 7733248 | tf_op jit(solution)/shard_map/input_projection/dot_general | solution.py:39
  90.7 0.0 copy-done.4
  90.7 0.8 copy.15
  91.5 6.4 %all-to-all-start = ((bf16[3,8,16,512]{3,2,0,1:T(8,128)(2,1)}), bf16[3,8,16,512]{3,2,0,1:T(8,128)(2,1)S(1)}, u32[]{:S(2)}, u32[]{:S(2)}) async-start(bf16[3,8,16,512]{3,2,0,1:T(8,128)(2,1)} %copy.15), calls=%async_computation | async-start | bytes 786432 | tf_op jit(solution)/shard_map/projection_to_owner/all_to_all | solution.py:44
  97.9 0.0 all-gather.5.cloned.1.call-start
  97.9 0.0 copy-done.1
  97.9 3.2 %fusion.3 = bf16[8,16,2048]{2,1,0:T(8,128)(2,1)S(1)} fusion(bf16[1024,1024]{1,0:T(8,128)(2,1)S(1)} %bitcast.118, bf16[1024,1024]{1,0:T(8,128)(2,1)} %bitcast.121, bf16[7,16,511]{2,1,0:T(8,128)(2,1)S(1)} %slice.145, bf16[8,16,512]{2,1,0:T(8,128)(2,1)} %copy-done.4, bf16[1024]{0:T(1024)(128)(2,1)S(1)} %pad.29.clone), kind=kOutput, calls=%fused_computation.7 | convolution fusion | flops 546570240 | bytes 4966176 | tf_op jit(solution)/shard_map/spectra/kdm,fm->kdf/dot_general | solution.py:73
  101.1 0.1 slice_convert_fusion.3
  101.2 6.1 %all-to-all-done = bf16[3,8,16,512]{3,2,0,1:T(8,128)(2,1)S(1)} async-done(((bf16[3,8,16,512]{3,2,0,1:T(8,128)(2,1)}), bf16[3,8,16,512]{3,2,0,1:T(8,128)(2,1)S(1)}, u32[]{:S(2)}, u32[]{:S(2)}) %all-to-all-start) | async-done | bytes 393248 | tf_op jit(solution)/shard_map/projection_to_owner/all_to_all | solution.py:44
  107.3 0.1 slice.141
  107.4 0.2 fusion.13
  107.7 0.4 add_convert_fusion
  108.0 2.0 convolution_convert_fusion
  110.1 0.1 slice_convert_fusion.2
  110.2 0.2 fusion.63
  110.4 0.2 fusion.64
  110.5 0.1 fusion.61
  110.7 0.1 fusion.62
  110.8 0.1 fusion.59
  110.9 0.1 fusion.60
  111.1 0.0 copy-start.2
  111.1 0.1 fusion.57
  111.1 0.1 fusion.58
  111.2 0.1 fusion.55
  111.3 0.1 fusion.56
  111.4 0.1 fusion.54
  111.5 0.1 fusion.53
  111.5 0.0 copy-start.3
  111.7 1.0 copy-done.2
  112.6 0.5 fusion.10
  113.1 9.8 %all_to_all.34 = bf16[8,16,512]{2,1,0:T(8,128)(2,1)} all-to-all(bf16[8,16,512]{2,1,0:T(8,128)(2,1)S(1)} %fusion.10), channel_id=1, replica_groups=mesh['ctx'=8,'chan'=32] {'ctx'}, dimensions={0} | all-to-all | bytes 262144 | tf_op jit(solution)/shard_map/gated_back_to_rows/all_to_all | solution.py:99
  122.9 0.0 all-gather.5.cloned.1.call-update
  123.0 0.0 copy-done.3
  123.0 0.7 copy.20
  123.7 44.2 %all_to_all.35 = bf16[128,32,128]{0,2,1:T(8,128)(2,1)S(1)} all-to-all(bf16[128,32,128]{0,2,1:T(8,128)(2,1)S(1)} %bitcast.116), channel_id=1, replica_groups=mesh['ctx'=8,'chan'=32] {'chan'}, dimensions={1} | all-to-all | bytes 2097152 | tf_op jit(solution)/shard_map/out_weight_columns/all_to_all | solution.py:32
  167.9 0.7 copy.21
  168.6 28.6 %all-gather.5.cloned.1.call-done = bf16[4096,512]{1,0:T(8,128)(2,1)} async-done(((bf16[128,512]{1,0:T(8,128)(2,1)}), bf16[4096,512]{1,0:T(8,128)(2,1)}) %all-gather.5.cloned.1.call-update) | async-done | bytes 4194320 | tf_op jit(solution)/shard_map/output_projection/all_gather | solution.py:102
  197.1 4.1 %convolution_convert_fusion.2 = bf16[512,128]{1,0:T(8,128)(2,1)} fusion(bf16[4096,512]{1,0:T(8,128)(2,1)} %all-gather.5.cloned.1.call-done, bf16[4096,128]{1,0:T(8,128)(2,1)S(1)} %bitcast.124), kind=kOutput, calls=%fused_computation.15 | convolution fusion | flops 536936448 | bytes 5373952 | tf_op jit(solution)/shard_map/output_projection/dot_general | solution.py:103
  (12 shorter events, 0.1 us)
Async XLA Ops:
  6.5 14.8 %copy-start = (bf16[4096,3,128]{2,0,1:T(8,128)(2,1)S(1)}, bf16[4096,3,128]{2,0,1:T(8,128)(2,1)}, u32[]{:S(2)}) copy-start(bf16[4096,3,128]{2,0,1:T(8,128)(2,1)} %param.7) | copy-start | bytes 9437188
  6.5 79.1 %all-gather.3.cloned.1.call-start = ((), (), s32[]{:S(2)}) async-start(), calls=%async_computation.4 | async-start | bytes 4325376 | tf_op jit(solution)/shard_map/input_projection/all_gather | solution.py:37
  9.1 15.2 %all-to-all-start.1 = ((bf16[8,16,512]{2,1,0:T(8,128)(2,1)}), bf16[8,16,512]{2,1,0:T(8,128)(2,1)S(1)}, u32[]{:S(2)}, u32[]{:S(2)}) async-start(bf16[8,16,512]{2,1,0:T(8,128)(2,1)} %bitcast.8), calls=%async_computation.1 | async-start | bytes 262144 | tf_op jit(solution)/shard_map/filter_to_owner/all_to_all | solution.py:35
  21.3 2.9 %copy-start.6 = (f32[128]{0:T(128)S(1)}, f32[128]{0:T(128)}, u32[]{:S(2)}) copy-start(f32[128]{0:T(128)} %param.9) | copy-start | bytes 1540
  21.3 3.0 %copy-start.5 = (bf16[3,3,128]{2,1,0:T(4,128)(2,1)S(1)}, bf16[3,3,128]{2,1,0:T(4,128)(2,1)}, u32[]{:S(2)}) copy-start(bf16[3,3,128]{2,1,0:T(4,128)(2,1)} %param.8) | copy-start | bytes 6916
  24.4 66.4 %copy-start.4 = (bf16[8,16,512]{2,1,0:T(8,128)(2,1)}, bf16[8,16,512]{2,1,0:T(8,128)(2,1)S(1)}, u32[]{:S(2)}) copy-start(bf16[8,16,512]{2,1,0:T(8,128)(2,1)S(1)} %all-to-all-done.1) | copy-start | bytes 393220
  85.6 12.3 %copy-start.1 = (bf16[32,32,1024]{2,1,0:T(8,128)(2,1)S(1)}, bf16[32,32,1024]{2,1,0:T(8,128)(2,1)}, u32[]{:S(2)}) copy-start(bf16[32,32,1024]{2,1,0:T(8,128)(2,1)} %get-tuple-element.15) | copy-start | bytes 6291460
  91.5 15.8 %all-to-all-start = ((bf16[3,8,16,512]{3,2,0,1:T(8,128)(2,1)}), bf16[3,8,16,512]{3,2,0,1:T(8,128)(2,1)S(1)}, u32[]{:S(2)}, u32[]{:S(2)}) async-start(bf16[3,8,16,512]{3,2,0,1:T(8,128)(2,1)} %copy.15), calls=%async_computation | async-start | bytes 786432 | tf_op jit(solution)/shard_map/projection_to_owner/all_to_all | solution.py:44
  97.9 99.3 %all-gather.5.cloned.1.call-start = ((), (), s32[]{:S(2)}) async-start(), calls=%async_computation.5 | async-start | bytes 4325376 | tf_op jit(solution)/shard_map/output_projection/all_gather | solution.py:102
  111.1 1.6 copy-start.2
  111.5 11.4 %copy-start.3 = (bf16[128,4096]{1,0:T(8,128)(2,1)S(1)}, bf16[128,4096]{1,0:T(8,128)(2,1)}, u32[]{:S(2)}) copy-start(bf16[128,4096]{1,0:T(8,128)(2,1)} %param.11) | copy-start | bytes 3145732
Sparse Core Ops, SparseCore 0:
  9.1 76.4 all-gather.2
  123.1 74.0 all-gather.4
where the time goes:
time: 209 us; the launch traced here: 208 us
  waiting for transfers between devices  96.6 us (46%)
  blocking collectives  54.1 us (26%)
  matrix products  14.9 us (7%)
  starting transfers between devices  13.9 us (7%)
  between operations  13.7 us (7%)
  local copies, waits for them, and re-layouts  8.15 us (4%)
  other arithmetic  6.84 us (3%)
    all_gather x1, waiting for transfers between devices, body(): inputs_t = lax.all_gather(inputs.T, 'chan', axis=0, tiled=True)  61.2 us
    all_to_all x1, blocking collectives, body(): w_cols = lax.all_to_all(w_out, 'chan', 1, 0, tiled=True)  44.2 us
    all_gather x1, waiting for transfers between devices, body(): gathered = lax.all_gather(gated_out, 'chan', axis=0, tiled=True)  28.6 us
    all_to_all x1, blocking collectives, body(): gated_out = lax.all_to_all(gated_out, 'ctx', 0, 0, tiled=True)  9.83 us
    all_to_all x1, starting transfers between devices, body(): taps_t = lax.all_to_all(taps_t, 'ctx', 0, 0, tiled=True)  7.48 us
    all_to_all x1, starting transfers between devices, body(): proj_t = lax.all_to_all(proj_t, 'ctx', 1, 1, tiled=True)  6.35 us
    all_to_all x1, waiting for transfers between devices, body(): proj_t = lax.all_to_all(proj_t, 'ctx', 1, 1, tiled=True)  6.07 us
    dot_general x1, matrix products, body(): lax.dot_general(w_flat, inputs_t, (((0,), (0,)), ((), ())), preferred_ele...  5.1 us
  transfers between devices with their start and end apart: 4, of which 3 were waited for; matrix products, arithmetic and copies ran while one was open for 7% of the time, Pallas kernels for 0%

commit v1 on v0

--- a/solution.py
+++ b/solution.py
@@ -5,6 +5,13 @@
 from jax.sharding import PartitionSpec as P
 
 KERNEL = 3
+
+
+def pack_the_task(packet):
+    val = jnp.concatenate(
+        lax.all_to_all(jnp.stack([packet] * lax.psum(1, "chan"), axis=0), "chan", 0, 0), axis=0
+    )
+    return val
 
 
 def dft_table(double_len):
@@ -99,7 +106,7 @@
         gated_out = lax.all_to_all(gated_out, "ctx", 0, 0, tiled=True)
         gated_out = gated_out.reshape(width_dev, span_len)
     with jax.named_scope("output_projection"):
-        gathered = lax.all_gather(gated_out, "chan", axis=0, tiled=True)
+        gathered = pack_the_task(gated_out)
         result = lax.dot_general(
             gathered, w_cols, (((0,), (0,)), ((), ())), preferred_element_type=jnp.float32
         ).astype(jnp.bfloat16)

time: 209 us -> 269 us (1.29)
  blocking collectives: 54.1 us -> 99.6 us
  starting transfers between devices: 13.9 us -> 24.1 us
  waiting for transfers between devices: 96.6 us -> 101 us
    all_to_all x2 -> x1, blocking collectives: 54.1 us -> 99.6 us  [pack_the_task(): lax.all_to_all(jnp.stack([packet] * lax.psum(1, 'chan'), axis=0), 'chan',...]
    all_to_all x0 -> x2, waiting for transfers between devices: none -> 32.7 us  [the longest x1 28 us: body(): w_cols = lax.all_to_all(w_out, 'chan', 1, 0, tiled=True)]
    all_gather x1 -> x0, waiting for transfers between devices: 28.6 us -> none  [body(): gathered = lax.all_gather(gated_out, 'chan', axis=0, tiled=True)]
    all_to_all x0 -> x2, starting transfers between devices: none -> 10.3 us  [the longest x1 6.9 us: body(): w_cols = lax.all_to_all(w_out, 'chan', 1, 0, tiled=True)]
  transfers between devices with their start and end apart: 4 -> 5, of which waited for: 3 -> 4; matrix products, arithmetic and copies ran while one was open for 7% -> 6% of each run, Pallas kernels for 0% -> 0%
where the time goes in v1:
time: 269 us; the launch traced here: 268 us
  waiting for transfers between devices  101 us (38%)
  blocking collectives  99.6 us (37%)
  starting transfers between devices  24.1 us (9%)
  between operations  13.7 us (5%)
  matrix products  13.4 us (5%)
  local copies, waits for them, and re-layouts  9.89 us (4%)
  other arithmetic  6.84 us (3%)
    all_to_all x1, blocking collectives, pack_the_task(): lax.all_to_all(jnp.stack([packet] * lax.psum(1, 'chan'), axis=0), 'chan',...  99.6 us
    all_gather x1, waiting for transfers between devices, body(): inputs_t = lax.all_gather(inputs.T, 'chan', axis=0, tiled=True)  61.2 us
    all_to_all x1, waiting for transfers between devices, body(): w_cols = lax.all_to_all(w_out, 'chan', 1, 0, tiled=True)  28 us
    all_to_all x1, starting transfers between devices, body(): taps_t = lax.all_to_all(taps_t, 'ctx', 0, 0, tiled=True)  7.48 us
    all_to_all x1, starting transfers between devices, body(): w_cols = lax.all_to_all(w_out, 'chan', 1, 0, tiled=True)  6.9 us
    all_to_all x1, starting transfers between devices, body(): proj_t = lax.all_to_all(proj_t, 'ctx', 1, 1, tiled=True)  6.35 us
    all_to_all x1, waiting for transfers between devices, body(): proj_t = lax.all_to_all(proj_t, 'ctx', 1, 1, tiled=True)  6.12 us
  transfers between devices with their start and end apart: 5, of which 4 were waited for; matrix products, arithmetic and copies ran while one was open for 6% of the time, Pallas kernels for 0%

profile of v1, /device:TPU:1, one launch (start us, length us, event | category | flops | bytes accessed | tf_op | source)
XLA Modules:
  0.0 268.2 jit_solution(13815494976643735436)
XLA Ops:
  6.5 0.0 copy-start
  6.5 0.0 all-gather.2.cloned.1.call-start
  6.5 0.7 all-gather.2.cloned.1.call-update
  7.3 1.9 copy.19
  9.1 7.5 %all-to-all-start.1 = ((bf16[8,16,512]{2,1,0:T(8,128)(2,1)}), bf16[8,16,512]{2,1,0:T(8,128)(2,1)S(1)}, u32[]{:S(2)}, u32[]{:S(2)}) async-start(bf16[8,16,512]{2,1,0:T(8,128)(2,1)} %bitcast.8), calls=%async_computation.1 | async-start | bytes 262144 | tf_op jit(solution)/shard_map/filter_to_owner/all_to_all | solution.py:42
  16.6 0.5 fusion.47
  17.2 0.6 fusion.50
  17.8 3.5 %negate_convert_fusion = (bf16[32,32,1024]{2,1,0:T(8,128)(2,1)}, bf16[32,32,1024]{2,1,0:T(8,128)(2,1)}) fusion(f32[32,1024]{1,0:T(8,128)S(1)} %get-tuple-element.22, f32[32,1024]{1,0:T(8,128)S(1)} %get-tuple-element.21, f32[32,1024]{1,0:T(8,128)S(1)} %get-tuple-element.23, f32[32,1024]{1,0:T(8,128)S(1)} %get-tuple-element.20), kind=kLoop, calls=%fused_computation.5 | loop fusion | flops 9437184 | bytes 4718592 | tf_op jit(solution)/shard_map/convert.44
  21.3 0.0 copy-start.6
  21.3 0.0 copy-start.5
  21.3 0.0 copy-done
  21.3 2.9 %copy.14 = bf16[4096,3,128]{0,2,1:T(8,128)(2,1)} copy(bf16[4096,3,128]{2,0,1:T(8,128)(2,1)S(1)} %copy-done) | data formatting | bytes 6291456 | tf_op args[1]
  24.2 0.0 copy-done.6
  24.2 0.1 dynamic_slice.7
  24.3 0.0 copy-done.5
  24.3 0.1 fusion.70
  24.3 0.0 all-to-all-done.1
  24.4 0.0 copy-start.4
  24.4 0.1 slice.145
  24.5 61.2 %all-gather.2.cloned.1.call-done = bf16[4096,512]{0,1:T(8,128)(2,1)} async-done(((bf16[128,512]{0,1:T(8,128)(2,1)}), bf16[4096,512]{0,1:T(8,128)(2,1)}) %all-gather.2.cloned.1.call-update) | async-done | bytes 4194320 | tf_op jit(solution)/shard_map/input_projection/all_gather | solution.py:44
  85.6 0.0 copy-start.1
  85.6 5.1 %convolution_convert_fusion.1 = bf16[384,512]{1,0:T(8,128)(2,1)S(1)} fusion(bf16[4096,384]{0,1:T(8,128)(2,1)} %bitcast.120, bf16[4096,512]{0,1:T(8,128)(2,1)} %all-gather.2.cloned.1.call-done), kind=kOutput, calls=%fused_computation.11 | convolution fusion | flops 1610809344 | bytes 7733248 | tf_op jit(solution)/shard_map/input_projection/dot_general | solution.py:46
  90.7 0.0 copy-done.4
  90.7 0.8 copy.15
  91.5 6.4 %all-to-all-start = ((bf16[3,8,16,512]{3,2,0,1:T(8,128)(2,1)}), bf16[3,8,16,512]{3,2,0,1:T(8,128)(2,1)S(1)}, u32[]{:S(2)}, u32[]{:S(2)}) async-start(bf16[3,8,16,512]{3,2,0,1:T(8,128)(2,1)} %copy.15), calls=%async_computation | async-start | bytes 786432 | tf_op jit(solution)/shard_map/projection_to_owner/all_to_all | solution.py:51
  97.9 0.0 copy-done.1
  97.9 3.2 %fusion.3 = bf16[8,16,2048]{2,1,0:T(8,128)(2,1)S(1)} fusion(bf16[1024,1024]{1,0:T(8,128)(2,1)S(1)} %bitcast.121, bf16[1024,1024]{1,0:T(8,128)(2,1)} %bitcast.124, bf16[7,16,511]{2,1,0:T(8,128)(2,1)S(1)} %slice.145, bf16[8,16,512]{2,1,0:T(8,128)(2,1)} %copy-done.4, bf16[1024]{0:T(1024)(128)(2,1)S(1)} %pad.29.clone), kind=kOutput, calls=%fused_computation.7 | convolution fusion | flops 546570240 | bytes 4966176 | tf_op jit(solution)/shard_map/spectra/kdm,fm->kdf/dot_general | solution.py:80
  101.1 0.1 slice_convert_fusion.3
  101.2 6.1 %all-to-all-done = bf16[3,8,16,512]{3,2,0,1:T(8,128)(2,1)S(1)} async-done(((bf16[3,8,16,512]{3,2,0,1:T(8,128)(2,1)}), bf16[3,8,16,512]{3,2,0,1:T(8,128)(2,1)S(1)}, u32[]{:S(2)}, u32[]{:S(2)}) %all-to-all-start) | async-done | bytes 393248 | tf_op jit(solution)/shard_map/projection_to_owner/all_to_all | solution.py:51
  107.3 0.1 slice.141
  107.4 0.2 fusion.15
  107.7 0.4 add_convert_fusion
  108.0 2.0 convolution_convert_fusion
  110.1 0.1 slice_convert_fusion.2
  110.2 0.2 fusion.65
  110.4 0.2 fusion.66
  110.5 0.1 fusion.63
  110.7 0.1 fusion.64
  110.8 0.1 fusion.61
  110.9 0.1 fusion.62
  111.1 0.0 copy-start.2
  111.1 0.1 fusion.59
  111.2 0.1 fusion.60
  111.2 0.1 fusion.57
  111.3 0.1 fusion.58
  111.4 0.1 fusion.56
  111.5 0.1 fusion.55
  111.5 0.0 copy-start.3
  111.7 1.0 copy-done.2
  112.7 1.1 fusion.11
  113.8 3.4 %all-to-all-start.2 = ((bf16[8,16,512]{2,1,0:T(8,128)(2,1)}), bf16[8,16,512]{2,1,0:T(8,128)(2,1)S(1)}, u32[]{:S(2)}, u32[]{:S(2)}) async-start(bf16[8,16,512]{2,1,0:T(8,128)(2,1)} %fusion.11), calls=%async_computation.2 | async-start | bytes 262144 | tf_op jit(solution)/shard_map/gated_back_to_rows/all_to_all | solution.py:106
  117.2 0.0 copy-done.3
  117.2 0.7 copy.21
  117.8 1.3 copy.22
  119.2 4.7 %all-to-all-done.2 = bf16[8,16,512]{2,1,0:T(8,128)(2,1)S(1)} async-done(((bf16[8,16,512]{2,1,0:T(8,128)(2,1)}), bf16[8,16,512]{2,1,0:T(8,128)(2,1)S(1)}, u32[]{:S(2)}, u32[]{:S(2)}) %all-to-all-start.2) | async-done | bytes 131104 | tf_op jit(solution)/shard_map/gated_back_to_rows/all_to_all | solution.py:106
  123.9 6.9 %all-to-all-start.4 = ((bf16[128,32,128]{2,0,1:T(8,128)(2,1)}), bf16[128,32,128]{2,0,1:T(8,128)(2,1)S(1)}, u32[]{:S(2)}, u32[]{:S(2)}) async-start(bf16[128,32,128]{2,0,1:T(8,128)(2,1)} %copy.22), calls=%async_computation.4 | async-start | bytes 2097152 | tf_op jit(solution)/shard_map/out_weight_columns/all_to_all | solution.py:39
  130.8 0.1 copy.20
  130.9 28.0 %all-to-all-done.4 = bf16[128,32,128]{2,0,1:T(8,128)(2,1)S(1)} async-done(((bf16[128,32,128]{2,0,1:T(8,128)(2,1)}), bf16[128,32,128]{2,0,1:T(8,128)(2,1)S(1)}, u32[]{:S(2)}, u32[]{:S(2)}) %all-to-all-start.4) | async-done | bytes 1048608 | tf_op jit(solution)/shard_map/out_weight_columns/all_to_all | solution.py:39
  158.9 0.9 stack.48
  159.9 99.6 %all_to_all.36 = bf16[32,128,512]{1,2,0:T(8,128)(2,1)S(1)} all-to-all(bf16[32,128,512]{1,2,0:T(8,128)(2,1)S(1)} %stack.48), channel_id=1, replica_groups=mesh['ctx'=8,'chan'=32] {'chan'}, dimensions={0} | all-to-all | bytes 8388608 | tf_op jit(solution)/shard_map/output_projection/all_to_all | solution.py:12
  259.5 1.9 fusion.10
  (12 shorter events, 0.1 us)
Async XLA Ops:
  6.5 14.7 %copy-start = (bf16[4096,3,128]{2,0,1:T(8,128)(2,1)S(1)}, bf16[4096,3,128]{2,0,1:T(8,128)(2,1)}, u32[]{:S(2)}) copy-start(bf16[4096,3,128]{2,0,1:T(8,128)(2,1)} %param.7) | copy-start | bytes 9437188
  6.5 79.1 %all-gather.2.cloned.1.call-start = ((), (), s32[]{:S(2)}) async-start(), calls=%async_computation.5 | async-start | bytes 4325376 | tf_op jit(solution)/shard_map/input_projection/all_gather | solution.py:44
  9.1 15.2 %all-to-all-start.1 = ((bf16[8,16,512]{2,1,0:T(8,128)(2,1)}), bf16[8,16,512]{2,1,0:T(8,128)(2,1)S(1)}, u32[]{:S(2)}, u32[]{:S(2)}) async-start(bf16[8,16,512]{2,1,0:T(8,128)(2,1)} %bitcast.8), calls=%async_computation.1 | async-start | bytes 262144 | tf_op jit(solution)/shard_map/filter_to_owner/all_to_all | solution.py:42
  21.3 2.9 %copy-start.6 = (f32[128]{0:T(128)S(1)}, f32[128]{0:T(128)}, u32[]{:S(2)}) copy-start(f32[128]{0:T(128)} %param.9) | copy-start | bytes 1540
  21.3 3.0 %copy-start.5 = (bf16[3,3,128]{2,1,0:T(4,128)(2,1)S(1)}, bf16[3,3,128]{2,1,0:T(4,128)(2,1)}, u32[]{:S(2)}) copy-start(bf16[3,3,128]{2,1,0:T(4,128)(2,1)} %param.8) | copy-start | bytes 6916
  24.4 66.4 %copy-start.4 = (bf16[8,16,512]{2,1,0:T(8,128)(2,1)}, bf16[8,16,512]{2,1,0:T(8,128)(2,1)S(1)}, u32[]{:S(2)}) copy-start(bf16[8,16,512]{2,1,0:T(8,128)(2,1)S(1)} %all-to-all-done.1) | copy-start | bytes 393220
  85.6 12.2 %copy-start.1 = (bf16[32,32,1024]{2,1,0:T(8,128)(2,1)S(1)}, bf16[32,32,1024]{2,1,0:T(8,128)(2,1)}, u32[]{:S(2)}) copy-start(bf16[32,32,1024]{2,1,0:T(8,128)(2,1)} %get-tuple-element.15) | copy-start | bytes 6291460
  91.5 15.8 %all-to-all-start = ((bf16[3,8,16,512]{3,2,0,1:T(8,128)(2,1)}), bf16[3,8,16,512]{3,2,0,1:T(8,128)(2,1)S(1)}, u32[]{:S(2)}, u32[]{:S(2)}) async-start(bf16[3,8,16,512]{3,2,0,1:T(8,128)(2,1)} %copy.15), calls=%async_computation | async-start | bytes 786432 | tf_op jit(solution)/shard_map/projection_to_owner/all_to_all | solution.py:51
  111.1 1.6 copy-start.2
  111.5 5.6 %copy-start.3 = (bf16[128,4096]{1,0:T(8,128)(2,1)S(1)}, bf16[128,4096]{1,0:T(8,128)(2,1)}, u32[]{:S(2)}) copy-start(bf16[128,4096]{1,0:T(8,128)(2,1)} %param.11) | copy-start | bytes 3145732
  113.8 10.1 %all-to-all-start.2 = ((bf16[8,16,512]{2,1,0:T(8,128)(2,1)}), bf16[8,16,512]{2,1,0:T(8,128)(2,1)S(1)}, u32[]{:S(2)}, u32[]{:S(2)}) async-start(bf16[8,16,512]{2,1,0:T(8,128)(2,1)} %fusion.11), calls=%async_computation.2 | async-start | bytes 262144 | tf_op jit(solution)/shard_map/gated_back_to_rows/all_to_all | solution.py:106
  123.9 35.0 %all-to-all-start.4 = ((bf16[128,32,128]{2,0,1:T(8,128)(2,1)}), bf16[128,32,128]{2,0,1:T(8,128)(2,1)S(1)}, u32[]{:S(2)}, u32[]{:S(2)}) async-start(bf16[128,32,128]{2,0,1:T(8,128)(2,1)} %copy.22), calls=%async_computation.4 | async-start | bytes 2097152 | tf_op jit(solution)/shard_map/out_weight_columns/all_to_all | solution.py:39
Sparse Core Ops, SparseCore 0:
  9.1 76.4 all-gather.1
